TPU v7x, 32 devices: a whole 2x2x4 slice. The times are simulated.
32 devices in a mesh: leaf: 4 (over x, core), front: 8 (over z, y).
Axes of the slice: x: 2, y: 2, z: 4, core: 2. Of those that a mesh axis runs over, the one named last changes fastest.
Arguments:
- leaf_field: float32 [64, 128, 4, 128], P(None, ('leaf', 'front')), may hold values from -4 to 4
- leaf_source: float32 [64, 128, 4, 128], P(None, ('leaf', 'front')), may hold values from -6 to 6
- wave_squared: float32 [128, 4, 128], P(('leaf', 'front')), may hold values from 0.5 to 3
- coupling_map: int32 [32, 512], P(('leaf', 'front')), may hold values from 0 to 255
- front_rhs: float32 [64, 2048], P(None, 'front'), may hold values from -6 to 6
- row_order: int32 [2048], P('front'), may hold values from 0 to 2047, each once
- lower_panels: bfloat16 [2048, 2048], P(None, 'front'), may hold values from -0.125 to 0.125
- inverse_slots: float32 [4096, 512], P('front'), as said below
- panel_owners: int32 [4], replicated, may hold values from 0 to 7, as said below
Outputs:
- leaf_residual: float32 [64, 128, 4, 128], P(None, ('leaf', 'front'))
- solved_blocks: float32 [64, 2048], replicated
- reduced_rhs: float32 [64, 2048], P(None, 'front')
Inputs may be any that keep to these rules, and one draw needn't show every extreme that they name: `panel_owners`: 4 distinct indices of the front axis, always including 0 and 7. `inverse_slots`: each slot of 512 rows is lower triangular with diagonal entries between 0.5 and 1.5.
All inputs are finite; a program needn't handle non-finite values.
Results may differ from a plain program's by a relative error of at most 0.0019.
Values sent between devices are 32-bit elements; how exact they have to be, the bound alone decides.
No kernel may reach another device: no remote copies, remote signals or barrier semaphores. Data moves between devices by JAX's collectives and lax.ppermute only.
A program may use at most 64 MiB of HBM per device.

v0:
```python
import jax
import jax.numpy as jnp
from jax import lax
from jax.sharding import PartitionSpec as P

centre_weight = 128.0 / 30.0
face_weight = 14.0 / 30.0
cycle_weights = (0.0, 14.0 / 30.0, 3.0 / 30.0, 1.0 / 30.0)


def spread(x, axis, root):
    mine = lax.axis_index(axis) == root
    return lax.psum(jnp.where(mine, x, jnp.zeros_like(x)), axis)


def apply_operator(field, wave):
    lead = field.ndim - 3
    padded = jnp.pad(field, [(0, 0)] * lead + [(1, 1)] * 3)
    extent_x, extent_y, extent_z = field.shape[-3:]
    beside = jnp.zeros_like(field)
    for step_x in (-1, 0, 1):
        for step_y in (-1, 0, 1):
            for step_z in (-1, 0, 1):
                distance = abs(step_x) + abs(step_y) + abs(step_z)
                if distance == 0:
                    continue
                window = padded[
                    ...,
                    1 + step_x : 1 + step_x + extent_x,
                    1 + step_y : 1 + step_y + extent_y,
                    1 + step_z : 1 + step_z + extent_z,
                ]
                beside = beside + cycle_weights[distance] * window
    return (centre_weight - wave) * field - beside


def apply_inverse(block, inverse):
    return lax.dot_general(
        block,
        inverse,
        (((1,), (1,)), ((), ())),
        precision=lax.Precision.HIGHEST,
        preferred_element_type=jnp.float32,
    )


def per_device(
    leaf_field,
    leaf_source,
    wave_squared,
    coupling_map,
    front_rhs,
    row_order,
    lower_panels,
    inverse_slots,
    panel_owners,
):
    residual = leaf_source - apply_operator(leaf_field, wave_squared)
    rhs_count = residual.shape[0]
    face = residual[:, -1].reshape(rhs_count, -1)
    rows_here = front_rhs.shape[1]
    hits = (coupling_map[0][:, None] == jnp.arange(rows_here, dtype=jnp.int32)[None, :]).astype(
        jnp.float32
    )
    coupled = face_weight * jnp.dot(
        face, hits, precision=lax.Precision.HIGHEST, preferred_element_type=jnp.float32
    )
    width = inverse_slots.shape[1]
    panel_count = lower_panels.shape[0] // width
    leading = 1.0
    reduced = front_rhs + lax.psum(coupled, "leaf")
    solved_list = []
    for panel in range(panel_count):
        wanted = panel * width + jnp.arange(width, dtype=jnp.int32)
        picker = (row_order[:, None] == wanted[None, :]).astype(jnp.float32)
        partial_block = jnp.dot(
            reduced, picker, precision=lax.Precision.HIGHEST, preferred_element_type=jnp.float32
        )
        block = lax.psum(partial_block, "front")
        own_solve = apply_inverse(block, inverse_slots)
        solved = spread(own_solve, "front", panel_owners[panel])
        solved_list.append(solved)
        solved_half = solved.astype(jnp.bfloat16)
        update = jnp.dot(
            solved_half,
            lower_panels[panel * width : (panel + 1) * width],
            preferred_element_type=jnp.float32,
        )
        keep = (row_order >= (panel + 1) * width).astype(jnp.float32)
        reduced = reduced - leading * (update * keep[None, :])
    return (residual, jnp.concatenate(solved_list, axis=1), reduced)


def solution(mesh):
    return jax.shard_map(
        per_device,
        mesh=mesh,
        in_specs=(
            P(None, ("leaf", "front"), None, None),
            P(None, ("leaf", "front"), None, None),
            P(("leaf", "front"), None, None),
            P(("leaf", "front"), None),
            P(None, "front"),
            P("front"),
            P(None, "front"),
            P("front", None),
            P(),
        ),
        out_specs=(P(None, ("leaf", "front"), None, None), P(), P(None, "front")),
        check_vma=False,
    )
```

profile of v0, /device:TPU:0, one launch (start us, length us, event | category | flops | bytes accessed | tf_op | source)
XLA Modules:
  0.0 651.4 jit_solution(8520964305867727912)
XLA Ops:
  8.0 10.8 %fusion.56 = f32[64,4,4,128]{3,2,1,0:T(4,128)S(1)} fusion(f32[64,4,4,128]{3,2,1,0:T(4,128)} %param.10, f32[64,4,4,128]{3,2,1,0:T(4,128)} %param.9, f32[4,4,128]{2,1,0:T(4,128)S(1)} %broadcast_subtract_fusion), kind=kLoop, calls=%fused_computation.91 | loop fusion | flops 7077888 | bytes 1581056 | tf_op jit(solution)/shard_map/sub | solution.py:58
  18.9 1.0 convolution_multiply_fusion
  19.9 34.3 %all-reduce.11.cloned.1.call-done = f32[64,256]{1,0:T(8,128)} async-done(((f32[64,256]{1,0:T(8,128)}), f32[64,256]{1,0:T(8,128)}) %all-reduce.11.cloned.1.call-update) | async-done | bytes 65552 | tf_op jit(solution)/shard_map/psum | solution.py:71
  54.3 0.8 add.153
  55.1 1.0 fusion.57
  57.5 71.1 %all-reduce.13.cloned.1.call-done = f32[64,512]{1,0:T(8,128)} async-done(((f32[64,512]{1,0:T(8,128)}), f32[64,512]{1,0:T(8,128)}) %all-reduce.13.cloned.1.call-update) | async-done | bytes 131088 | tf_op jit(solution)/shard_map/psum | solution.py:79
  128.6 2.7 convolution_select_fusion.3
  131.4 70.6 %all-reduce.15.cloned.1.call-done = f32[64,512]{1,0:T(8,128)} async-done(((f32[64,512]{1,0:T(8,128)}), f32[64,512]{1,0:T(8,128)}) %all-reduce.15.cloned.1.call-update) | async-done | bytes 131088 | tf_op jit(solution)/shard_map/psum | solution.py:13
  202.0 1.1 fusion.3
  203.1 1.0 fusion.62
  204.8 70.5 %all-reduce.17.cloned.1.call-done = f32[64,512]{1,0:T(8,128)} async-done(((f32[64,512]{1,0:T(8,128)}), f32[64,512]{1,0:T(8,128)}) %all-reduce.17.cloned.1.call-update) | async-done | bytes 131088 | tf_op jit(solution)/shard_map/psum | solution.py:79
  275.3 2.7 convolution_select_fusion.2
  278.1 70.5 %all-reduce.19.cloned.1.call-done = f32[64,512]{1,0:T(8,128)} async-done(((f32[64,512]{1,0:T(8,128)}), f32[64,512]{1,0:T(8,128)}) %all-reduce.19.cloned.1.call-update) | async-done | bytes 131088 | tf_op jit(solution)/shard_map/psum | solution.py:13
  348.6 1.1 fusion.2
  349.6 1.0 fusion.60
  351.4 70.4 %all-reduce.21.cloned.1.call-done = f32[64,512]{1,0:T(8,128)} async-done(((f32[64,512]{1,0:T(8,128)}), f32[64,512]{1,0:T(8,128)}) %all-reduce.21.cloned.1.call-update) | async-done | bytes 131088 | tf_op jit(solution)/shard_map/psum | solution.py:79
  421.9 2.7 convolution_select_fusion.1
  424.6 70.7 %all-reduce.23.cloned.1.call-done = f32[64,512]{1,0:T(8,128)} async-done(((f32[64,512]{1,0:T(8,128)}), f32[64,512]{1,0:T(8,128)}) %all-reduce.23.cloned.1.call-update) | async-done | bytes 131088 | tf_op jit(solution)/shard_map/psum | solution.py:13
  495.3 1.1 fusion.1
  496.5 1.0 fusion.58
  498.2 70.5 %all-reduce.25.cloned.1.call-done = f32[64,512]{1,0:T(8,128)} async-done(((f32[64,512]{1,0:T(8,128)}), f32[64,512]{1,0:T(8,128)}) %all-reduce.25.cloned.1.call-update) | async-done | bytes 131088 | tf_op jit(solution)/shard_map/psum | solution.py:79
  568.7 2.7 convolution_select_fusion
  571.4 70.7 %all-reduce.27.cloned.1.call-done = f32[64,512]{1,0:T(8,128)} async-done(((f32[64,512]{1,0:T(8,128)}), f32[64,512]{1,0:T(8,128)}) %all-reduce.27.cloned.1.call-update) | async-done | bytes 131088 | tf_op jit(solution)/shard_map/psum | solution.py:13
  642.2 1.8 pad_maximum_fusion
  (48 shorter events, 2.9 us)
Async XLA Ops:
  7.2 121.4 %copy-start = (f32[512,512]{1,0:T(8,128)S(1)}, f32[512,512]{1,0:T(8,128)}, u32[]{:S(2)}) copy-start(f32[512,512]{1,0:T(8,128)} %param.16) | copy-start | bytes 3145732
  7.2 11.7 %copy-start.10 = (s32[1,512]{1,0:T(1,128)S(1)}, s32[1,512]{1,0:T(1,128)}, u32[]{:S(2)}) copy-start(s32[1,512]{1,0:T(1,128)} %param.12) | copy-start | bytes 6148
  7.2 47.1 %all-reduce.11.cloned.1.call-start = ((), (), s32[]{:S(2)}) async-start(), calls=%async_computation | async-start | bytes 131072 | tf_op jit(solution)/shard_map/psum | solution.py:71
  8.0 46.2 %copy-start.7 = (f32[64,256]{1,0:T(8,128)S(1)}, f32[64,256]{1,0:T(8,128)}, u32[]{:S(2)}) copy-start(f32[64,256]{1,0:T(8,128)} %param.13) | copy-start | bytes 196612
  8.0 47.1 %copy-start.8 = (s32[256]{0:T(256)S(1)}, s32[256]{0:T(256)}, u32[]{:S(2)}) copy-start(s32[256]{0:T(256)} %param.14) | copy-start | bytes 3076
  8.0 48.2 %copy-start.9 = (s32[4]{0:T(128)S(1)}, s32[4]{0:T(128)}, u32[]{:S(2)}) copy-start(s32[4]{0:T(128)} %param.17) | copy-start | bytes 52
  18.8 112.5 %copy-start.2 = (f32[64,4,4,128]{3,2,1,0:T(4,128)}, f32[64,4,4,128]{3,2,1,0:T(4,128)S(1)}, u32[]{:S(2)}) copy-start(f32[64,4,4,128]{3,2,1,0:T(4,128)S(1)} %fusion.56) | copy-start | bytes 1572868
  19.9 182.2 %copy-start.1 = (bf16[2048,256]{1,0:T(8,128)(2,1)S(1)}, bf16[2048,256]{1,0:T(8,128)(2,1)}, u32[]{:S(2)}) copy-start(bf16[2048,256]{1,0:T(8,128)(2,1)} %param.15) | copy-start | bytes 3145732
  19.9 108.7 %all-reduce.13.cloned.1.call-start = ((), (), s32[]{:S(2)}) async-start(), calls=%async_computation.1 | async-start | bytes 262144 | tf_op jit(solution)/shard_map/psum | solution.py:79
  56.2 145.8 %all-reduce.15.cloned.1.call-start = ((), (), s32[]{:S(2)}) async-start(), calls=%async_computation.2 | async-start | bytes 262144 | tf_op jit(solution)/shard_map/psum | solution.py:13
  131.3 144.0 %all-reduce.17.cloned.1.call-start = ((), (), s32[]{:S(2)}) async-start(), calls=%async_computation.3 | async-start | bytes 262144 | tf_op jit(solution)/shard_map/psum | solution.py:79
  204.2 144.4 %all-reduce.19.cloned.1.call-start = ((), (), s32[]{:S(2)}) async-start(), calls=%async_computation.4 | async-start | bytes 262144 | tf_op jit(solution)/shard_map/psum | solution.py:13
  278.0 143.8 %all-reduce.21.cloned.1.call-start = ((), (), s32[]{:S(2)}) async-start(), calls=%async_computation.5 | async-start | bytes 262144 | tf_op jit(solution)/shard_map/psum | solution.py:79
  350.7 144.6 %all-reduce.23.cloned.1.call-start = ((), (), s32[]{:S(2)}) async-start(), calls=%async_computation.6 | async-start | bytes 262144 | tf_op jit(solution)/shard_map/psum | solution.py:13
  424.6 144.2 %all-reduce.25.cloned.1.call-start = ((), (), s32[]{:S(2)}) async-start(), calls=%async_computation.7 | async-start | bytes 262144 | tf_op jit(solution)/shard_map/psum | solution.py:79
  495.3 146.9 %copy-start.3 = (f32[64,512]{1,0:T(8,128)S(1)}, f32[64,512]{1,0:T(8,128)}, u32[]{:S(2)}) copy-start(f32[64,512]{1,0:T(8,128)} %all-reduce.15.cloned.1.call-done) | copy-start | bytes 393220
  495.3 146.9 %copy-start.4 = (f32[64,512]{1,0:T(8,128)S(1)}, f32[64,512]{1,0:T(8,128)}, u32[]{:S(2)}) copy-start(f32[64,512]{1,0:T(8,128)} %all-reduce.19.cloned.1.call-done) | copy-start | bytes 393220
  495.3 146.9 %copy-start.5 = (f32[64,512]{1,0:T(8,128)S(1)}, f32[64,512]{1,0:T(8,128)}, u32[]{:S(2)}) copy-start(f32[64,512]{1,0:T(8,128)} %all-reduce.23.cloned.1.call-done) | copy-start | bytes 393220
  497.5 144.7 %all-reduce.27.cloned.1.call-start = ((), (), s32[]{:S(2)}) async-start(), calls=%async_computation.8 | async-start | bytes 262144 | tf_op jit(solution)/shard_map/psum | solution.py:13
  642.2 1.8 copy-start.6
Sparse Core Ops, SparseCore 0:
  20.0 34.1 all-reduce.10
  58.2 70.3 all-reduce.12
  132.5 69.4 all-reduce.14
  205.8 69.4 all-reduce.16
  279.1 69.4 all-reduce.18
  352.3 69.4 all-reduce.20
  425.8 69.4 all-reduce.22
  499.2 69.4 all-reduce.24
  572.7 69.4 all-reduce.26
where the time goes:
time: 652 us; the launch traced here: 651 us
  waiting for transfers between devices  600 us (92%)
  matrix products  20 us (3%)
  between operations  16.5 us (3%)
  other arithmetic  14.2 us (2%)
    psum x4, waiting for transfers between devices, spread(): return lax.psum(jnp.where(mine, x, jnp.zeros_like(x)), axis)  283 us
    psum x4, waiting for transfers between devices, per_device(): block = lax.psum(partial_block, 'front')  283 us
    psum x1, waiting for transfers between devices, per_device(): reduced = front_rhs + lax.psum(coupled, 'leaf')  34.3 us
  transfers between devices with their start and end apart: 9, of which 9 were waited for; matrix products, arithmetic and copies ran while one was open for 0% of the time, Pallas kernels for 0%

commit v1 on v0

--- a/solution.py
+++ b/solution.py
@@ -76,7 +76,7 @@
         partial_block = jnp.dot(
             reduced, picker, precision=lax.Precision.HIGHEST, preferred_element_type=jnp.float32
         )
-        block = lax.psum(partial_block, "front")
+        block = jnp.sum(lax.all_gather(partial_block, "front"), axis=0)
         own_solve = apply_inverse(block, inverse_slots)
         solved = spread(own_solve, "front", panel_owners[panel])
         solved_list.append(solved)

time: 652 us -> 526 us (0.81)
  waiting for transfers between devices: 600 us -> 471 us
    psum x4 -> x0, waiting for transfers between devices: 283 us -> none  [per_device(): block = lax.psum(partial_block, 'front')]
    all_gather x0 -> x4, waiting for transfers between devices: none -> 157 us  [per_device(): block = jnp.sum(lax.all_gather(partial_block, 'front'), axis=0)]
where the time goes in v1:
time: 526 us; the launch traced here: 525 us
  waiting for transfers between devices  471 us (90%)
  other arithmetic  20.4 us (4%)
  between operations  16.4 us (3%)
  matrix products  16.3 us (3%)
    psum x4, waiting for transfers between devices, spread(): return lax.psum(jnp.where(mine, x, jnp.zeros_like(x)), axis)  279 us
    all_gather x4, waiting for transfers between devices, per_device(): block = jnp.sum(lax.all_gather(partial_block, 'front'), axis=0)  157 us
    psum x1, waiting for transfers between devices, per_device(): reduced = front_rhs + lax.psum(coupled, 'leaf')  34.3 us
    sub x1, other arithmetic, per_device(): residual = leaf_source - apply_operator(leaf_field, wave_squared)  11.6 us
  transfers between devices with their start and end apart: 9, of which 9 were waited for; matrix products, arithmetic and copies ran while one was open for 0% of the time, Pallas kernels for 0%

profile of v1, /device:TPU:0, one launch (start us, length us, event | category | flops | bytes accessed | tf_op | source)
XLA Modules:
  0.0 525.4 jit_solution(6513122682947617114)
XLA Ops:
  8.0 11.6 %fusion.56 = f32[64,4,4,128]{3,2,1,0:T(4,128)S(1)} fusion(f32[64,4,4,128]{3,2,1,0:T(4,128)} %param.10, f32[64,4,4,128]{3,2,1,0:T(4,128)} %param.9, f32[4,4,128]{2,1,0:T(4,128)S(1)} %broadcast_subtract_fusion), kind=kLoop, calls=%fused_computation.91 | loop fusion | flops 7077888 | bytes 1581056 | tf_op jit(solution)/shard_map/sub | solution.py:58
  20.7 34.3 %all-reduce.7.cloned.1.call-done = f32[64,256]{1,0:T(8,128)} async-done(((f32[64,256]{1,0:T(8,128)}), f32[64,256]{1,0:T(8,128)}) %all-reduce.7.cloned.1.call-update) | async-done | bytes 65552 | tf_op jit(solution)/shard_map/psum | solution.py:71
  58.4 39.7 %all-gather.9.cloned.1.call-done = f32[512,512]{1,0:T(8,128)} async-done(((f32[64,512]{1,0:T(8,128)}), f32[512,512]{1,0:T(8,128)}) %all-gather.9.cloned.1.call-update) | async-done | bytes 1048592 | tf_op jit(solution)/shard_map/all_gather | solution.py:79
  98.0 1.4 reduce_sum.36
  99.5 1.8 convolution_select_fusion.3
  101.3 69.8 %all-reduce.9.cloned.1.call-done = f32[64,512]{1,0:T(8,128)} async-done(((f32[64,512]{1,0:T(8,128)}), f32[64,512]{1,0:T(8,128)}) %all-reduce.9.cloned.1.call-update) | async-done | bytes 131088 | tf_op jit(solution)/shard_map/psum | solution.py:13
  171.1 1.1 fusion.3
  172.2 1.0 fusion.62
  173.9 39.2 %all-gather.11.cloned.1.call-done = f32[512,512]{1,0:T(8,128)} async-done(((f32[64,512]{1,0:T(8,128)}), f32[512,512]{1,0:T(8,128)}) %all-gather.11.cloned.1.call-update) | async-done | bytes 1048592 | tf_op jit(solution)/shard_map/all_gather | solution.py:79
  213.1 1.3 reduce_sum.37
  214.4 1.8 convolution_select_fusion.2
  216.3 69.8 %all-reduce.11.cloned.1.call-done = f32[64,512]{1,0:T(8,128)} async-done(((f32[64,512]{1,0:T(8,128)}), f32[64,512]{1,0:T(8,128)}) %all-reduce.11.cloned.1.call-update) | async-done | bytes 131088 | tf_op jit(solution)/shard_map/psum | solution.py:13
  286.0 1.1 fusion.2
  287.1 1.0 fusion.60
  288.8 39.2 %all-gather.13.cloned.1.call-done = f32[512,512]{1,0:T(8,128)} async-done(((f32[64,512]{1,0:T(8,128)}), f32[512,512]{1,0:T(8,128)}) %all-gather.13.cloned.1.call-update) | async-done | bytes 1048592 | tf_op jit(solution)/shard_map/all_gather | solution.py:79
  328.0 1.3 reduce_sum.38
  329.3 1.8 convolution_select_fusion.1
  331.2 69.9 %all-reduce.13.cloned.1.call-done = f32[64,512]{1,0:T(8,128)} async-done(((f32[64,512]{1,0:T(8,128)}), f32[64,512]{1,0:T(8,128)}) %all-reduce.13.cloned.1.call-update) | async-done | bytes 131088 | tf_op jit(solution)/shard_map/psum | solution.py:13
  401.1 1.1 fusion.1
  403.9 39.3 %all-gather.15.cloned.1.call-done = f32[512,512]{1,0:T(8,128)} async-done(((f32[64,512]{1,0:T(8,128)}), f32[512,512]{1,0:T(8,128)}) %all-gather.15.cloned.1.call-update) | async-done | bytes 1048592 | tf_op jit(solution)/shard_map/all_gather | solution.py:79
  443.2 1.4 reduce_sum.39
  444.5 1.8 convolution_select_fusion
  446.3 69.9 %all-reduce.15.cloned.1.call-done = f32[64,512]{1,0:T(8,128)} async-done(((f32[64,512]{1,0:T(8,128)}), f32[64,512]{1,0:T(8,128)}) %all-reduce.15.cloned.1.call-update) | async-done | bytes 131088 | tf_op jit(solution)/shard_map/psum | solution.py:13
  516.3 1.8 pad_maximum_fusion
  (52 shorter events, 6.8 us)
Async XLA Ops:
  7.2 92.3 %copy-start = (f32[512,512]{1,0:T(8,128)S(1)}, f32[512,512]{1,0:T(8,128)}, u32[]{:S(2)}) copy-start(f32[512,512]{1,0:T(8,128)} %param.16) | copy-start | bytes 3145732
  7.2 12.5 %copy-start.10 = (s32[1,512]{1,0:T(1,128)S(1)}, s32[1,512]{1,0:T(1,128)}, u32[]{:S(2)}) copy-start(s32[1,512]{1,0:T(1,128)} %param.12) | copy-start | bytes 6148
  7.2 47.8 %all-reduce.7.cloned.1.call-start = ((), (), s32[]{:S(2)}) async-start(), calls=%async_computation | async-start | bytes 131072 | tf_op jit(solution)/shard_map/psum | solution.py:71
  8.0 47.0 %copy-start.7 = (f32[64,256]{1,0:T(8,128)S(1)}, f32[64,256]{1,0:T(8,128)}, u32[]{:S(2)}) copy-start(f32[64,256]{1,0:T(8,128)} %param.13) | copy-start | bytes 196612
  8.0 47.9 %copy-start.8 = (s32[256]{0:T(256)S(1)}, s32[256]{0:T(256)}, u32[]{:S(2)}) copy-start(s32[256]{0:T(256)} %param.14) | copy-start | bytes 3076
  8.0 49.0 %copy-start.9 = (s32[4]{0:T(128)S(1)}, s32[4]{0:T(128)}, u32[]{:S(2)}) copy-start(s32[4]{0:T(128)} %param.17) | copy-start | bytes 52
  19.6 79.9 %copy-start.2 = (f32[64,4,4,128]{3,2,1,0:T(4,128)}, f32[64,4,4,128]{3,2,1,0:T(4,128)S(1)}, u32[]{:S(2)}) copy-start(f32[64,4,4,128]{3,2,1,0:T(4,128)S(1)} %fusion.56) | copy-start | bytes 1572868
  20.7 77.4 %all-gather.9.cloned.1.call-start = ((), (), s32[]{:S(2)}) async-start(), calls=%async_computation.5 | async-start | bytes 1179648 | tf_op jit(solution)/shard_map/all_gather | solution.py:79
  57.0 114.2 %all-reduce.9.cloned.1.call-start = ((), (), s32[]{:S(2)}) async-start(), calls=%async_computation.1 | async-start | bytes 262144 | tf_op jit(solution)/shard_map/psum | solution.py:13
  98.0 73.1 %copy-start.1 = (bf16[2048,256]{1,0:T(8,128)(2,1)S(1)}, bf16[2048,256]{1,0:T(8,128)(2,1)}, u32[]{:S(2)}) copy-start(bf16[2048,256]{1,0:T(8,128)(2,1)} %param.15) | copy-start | bytes 3145732
  101.3 111.8 %all-gather.11.cloned.1.call-start = ((), (), s32[]{:S(2)}) async-start(), calls=%async_computation.6 | async-start | bytes 1179648 | tf_op jit(solution)/shard_map/all_gather | solution.py:79
  173.3 112.7 %all-reduce.11.cloned.1.call-start = ((), (), s32[]{:S(2)}) async-start(), calls=%async_computation.2 | async-start | bytes 262144 | tf_op jit(solution)/shard_map/psum | solution.py:13
  216.2 111.8 %all-gather.13.cloned.1.call-start = ((), (), s32[]{:S(2)}) async-start(), calls=%async_computation.7 | async-start | bytes 1179648 | tf_op jit(solution)/shard_map/all_gather | solution.py:79
  288.2 112.9 %all-reduce.13.cloned.1.call-start = ((), (), s32[]{:S(2)}) async-start(), calls=%async_computation.3 | async-start | bytes 262144 | tf_op jit(solution)/shard_map/psum | solution.py:13
  331.1 112.1 %all-gather.15.cloned.1.call-start = ((), (), s32[]{:S(2)}) async-start(), calls=%async_computation.8 | async-start | bytes 1179648 | tf_op jit(solution)/shard_map/all_gather | solution.py:79
  403.2 113.1 %all-reduce.15.cloned.1.call-start = ((), (), s32[]{:S(2)}) async-start(), calls=%async_computation.4 | async-start | bytes 262144 | tf_op jit(solution)/shard_map/psum | solution.py:13
  443.2 73.1 %copy-start.3 = (f32[64,512]{1,0:T(8,128)S(1)}, f32[64,512]{1,0:T(8,128)}, u32[]{:S(2)}) copy-start(f32[64,512]{1,0:T(8,128)} %all-reduce.9.cloned.1.call-done) | copy-start | bytes 393220
  443.2 73.1 %copy-start.4 = (f32[64,512]{1,0:T(8,128)S(1)}, f32[64,512]{1,0:T(8,128)}, u32[]{:S(2)}) copy-start(f32[64,512]{1,0:T(8,128)} %all-reduce.11.cloned.1.call-done) | copy-start | bytes 393220
  443.2 73.1 %copy-start.5 = (f32[64,512]{1,0:T(8,128)S(1)}, f32[64,512]{1,0:T(8,128)}, u32[]{:S(2)}) copy-start(f32[64,512]{1,0:T(8,128)} %all-reduce.13.cloned.1.call-done) | copy-start | bytes 393220
  516.3 1.8 copy-start.6
Sparse Core Ops, SparseCore 0:
  20.8 34.1 all-reduce.6
  57.7 40.2 all-gather.8
  102.0 69.1 all-reduce.8
  173.7 39.3 all-gather.10
  216.9 69.1 all-reduce.10
  288.6 39.3 all-gather.12
  331.9 69.1 all-reduce.12
  403.8 39.3 all-gather.14
  447.1 69.1 all-reduce.14
